TPU v7x, 512 devices: a whole 4x8x8 slice. The times are simulated.
512 devices in a mesh: ctx: 64 (over x, y, core), tp: 8 (over z).
Axes of the slice: x: 4, y: 8, z: 8, core: 2. Of those that a mesh axis runs over, the one named last changes fastest.
Arguments:
- q_one: bfloat16 [16384, 8192], P('ctx', 'tp'), may hold values from -6 to 6
- k_one: bfloat16 [16384, 8192], P('ctx', 'tp'), may hold values from -40 to 40, as said below
- v_one: bfloat16 [16384, 8192], P('ctx', 'tp'), may hold values from -6 to 6
- mr_filter: bfloat16 [512, 128], P('tp'), may hold values from -3.535534 to 3.535534
- norm_gain: float32 [8192], P('tp'), may hold values from 0.1 to 1.9
- q_two: bfloat16 [16384, 8192], P('ctx', 'tp'), may hold values from -6 to 6
- k_two: bfloat16 [16384, 8192], P('ctx', 'tp'), may hold values from -6 to 6
- li_rates: float32 [16, 8192], P(None, 'tp'), may hold values from 1.5258789e-05 to 0.03
- li_residues: float32 [16, 8192], P(None, 'tp'), may hold values from -4 to 4
Outputs:
- mixed: bfloat16 [16384, 8192], P('ctx', 'tp')
Inputs may be any that keep to these rules, and one draw needn't show every extreme that they name: Each row of k_one has a scale of its own.
All inputs are finite; a program needn't handle non-finite values.
Results may differ from a plain program's by a relative error of at most 0.0057.
Values may be sent and summed in bfloat16 or wider, within the bound.
No kernel may reach another device: no remote copies, remote signals or barrier semaphores. Data moves between devices by JAX's collectives and lax.ppermute only.
A program may use at most 128 MiB of HBM per device.

v0:
```python
import jax
import jax.numpy as jnp
from jax import lax
from jax.sharding import PartitionSpec as P

D = 8192


def passed_along(value, axis, steps):
    count = lax.axis_size(axis)
    leading, last = (max(0, -steps), min(count, count - steps))
    return lax.ppermute(value, axis, [(source, source + steps) for source in range(leading, last)])


def join_states(earlier, later):
    return (earlier[0] * later[0], later[0] * earlier[1] + later[1])


def modal_parts(rates, residues, sub_len):
    norm_scale = jnp.sqrt(-jnp.expm1(-2.0 * rates))
    weights = residues * norm_scale
    lags = jnp.arange(sub_len).astype(jnp.float32)
    powers = jnp.exp(-rates[:, None, :] * lags[None, :, None])
    kernel = jnp.sum(weights[:, None, :] * powers, axis=0)
    lag_table = jnp.arange(sub_len)[:, None] - jnp.arange(sub_len)[None, :]
    toeplitz = jnp.where(
        (lag_table >= 0)[:, :, None], kernel[jnp.clip(lag_table, 0, sub_len - 1)], 0.0
    )
    closing_w = powers[:, ::-1, :]
    entry_w = weights[:, None, :] * powers * jnp.exp(-rates)[:, None, :]
    stride_decay = jnp.exp(-rates * sub_len)
    return (toeplitz, closing_w, entry_w, stride_decay)


def local_pass(signal, parts):
    toeplitz, closing_w, entry_w, stride_decay = parts
    inner = jnp.einsum("ijc,bjc->bic", toeplitz, signal, precision=lax.Precision.HIGHEST)
    closing = jnp.einsum("mjc,bjc->bmc", closing_w, signal, precision=lax.Precision.HIGHEST)
    decays = jnp.broadcast_to(stride_decay, closing.shape)
    _, states = lax.associative_scan(join_states, (decays, closing), axis=0)
    return (inner, states)


def finish(inner, states, incoming, rates, parts):
    entry_w = parts[2]
    sub_len = inner.shape[1]
    prior = jnp.concatenate([jnp.zeros_like(states[:1]), states[:-1]], axis=0)
    count = jnp.arange(inner.shape[0]).astype(jnp.float32)[:, None, None]
    prior = prior + jnp.exp(-rates[None] * (sub_len * count)) * incoming[None]
    return inner + jnp.einsum("mic,bmc->bic", entry_w, prior, precision=lax.Precision.HIGHEST)


def short_conv(extended, mr_filter):
    channels = extended.shape[1]
    group_ch = channels // mr_filter.shape[0]
    chan_taps = jnp.repeat(mr_filter, group_ch, axis=0).T
    kernel = chan_taps[::-1][:, None, :]
    result = lax.conv_general_dilated(
        extended[None],
        kernel,
        (1,),
        "VALID",
        dimension_numbers=("NWC", "WIO", "NWC"),
        feature_group_count=channels,
        precision=lax.Precision.HIGHEST,
        preferred_element_type=jnp.float32,
    )
    return result[0]


def on_device(q_one, k_one, v_one, mr_filter, norm_gain, q_two, k_two, li_rates, li_residues):
    length, channels = q_one.shape
    taps = mr_filter.shape[1]
    u_one = (k_one.astype(jnp.float32) * v_one.astype(jnp.float32)).astype(jnp.bfloat16)
    previous = passed_along(u_one[length - taps + 1 :], "ctx", 1)
    extended = jnp.concatenate([previous, u_one], axis=0)
    conv_one = short_conv(extended, mr_filter)
    z_one = q_one.astype(jnp.float32) * conv_one
    squares = lax.psum(jnp.sum(z_one * z_one, axis=1), "tp")
    scaled = z_one * lax.rsqrt(squares / D + 1e-06)[:, None] * norm_gain[None, :]
    u_two = (k_two.astype(jnp.float32) * scaled).astype(jnp.bfloat16)
    sub_len = min(32, length)
    devices = lax.axis_size("ctx")
    per_device = channels // devices
    gathered = lax.all_to_all(u_two, "ctx", split_axis=1, concat_axis=0, tiled=True)
    offset = lax.axis_index("ctx") * per_device
    rates = lax.dynamic_slice_in_dim(li_rates, offset, per_device, 1)
    residues = lax.dynamic_slice_in_dim(li_residues, offset, per_device, 1)
    parts = modal_parts(rates, residues, sub_len)
    full_len = gathered.shape[0]
    signal = gathered.astype(jnp.float32).reshape(full_len // sub_len, sub_len, per_device)
    inner, states = local_pass(signal, parts)
    modes = rates.shape[0]
    result = finish(inner, states, jnp.zeros((modes, per_device), jnp.float32), rates, parts)
    conv_two = lax.all_to_all(
        result.reshape(full_len, per_device), "ctx", split_axis=0, concat_axis=1, tiled=True
    )
    return (q_two.astype(jnp.float32) * conv_two).astype(jnp.bfloat16)


def solution(mesh):
    in_specs = (
        P("ctx", "tp"),
        P("ctx", "tp"),
        P("ctx", "tp"),
        P("tp", None),
        P("tp"),
        P("ctx", "tp"),
        P("ctx", "tp"),
        P(None, "tp"),
        P(None, "tp"),
    )
    out_specs = P("ctx", "tp")
    return jax.shard_map(
        on_device, mesh=mesh, in_specs=in_specs, out_specs=out_specs, check_vma=False
    )
```

profile of v0, /device:TPU:1, one launch (start us, length us, event | category | flops | bytes accessed | tf_op | source)
XLA Modules:
  0.0 273.4 jit_solution(8636405642247093626)
XLA Ops:
  0.0 1.4 multiply_convert_fusion.1
  1.5 4.6 %collective-permute-start = (bf16[127,1024]{1,0:T(8,128)(2,1)S(1)}, bf16[127,1024]{1,0:T(8,128)(2,1)S(1)}, u32[]{:S(2)}, u32[]{:S(2)}) collective-permute-start(bf16[127,1024]{1,0:T(8,128)(2,1)S(1)} %slice.258), channel_id=1, source_target_pairs={{0,8},{8,16},{16,24},{24,32},{32,40},{40,48},{48,56},{56,64},{64,7... | collective-permute-start | bytes 780296 | tf_op jit(solution)/shard_map/ppermute | solution.py:12
  8.2 2.4 collective-permute-done
  10.8 14.1 %fusion = f32[1,256,1024]{2,0,1:T(1,128)S(1)} fusion(bf16[128,1,1024]{2,1,0:T(2,128)(2,1)S(1)} %copy.107, bf16[1,383,1024]{2,1,0:T(8,128)(2,1)S(1)} %maximum_bitcast_fusion), kind=kOutput, calls=%fused_computation.1 | convolution fusion | flops 67108864 | bytes 2095104 | tf_op jit(solution)/shard_map/conv_general_dilated | solution.py:58
  25.2 18.2 %psum.7 = f32[256]{0:T(256)S(1)} all-reduce(f32[256]{0:T(256)S(1)} %multiply_reduce_fusion), channel_id=1, replica_groups=mesh['ctx'=64,'tp'=8] {'tp'}, use_global_device_ids=true, to_apply=%region_1.0 | all-reduce | flops 256 | bytes 2048 | tf_op jit(solution)/shard_map/psum | solution.py:79
  43.7 1.0 copy.108
  44.7 16.7 %all-to-all-start = ((bf16[256,64,16]{0,2,1:T(8,128)(2,1)}), bf16[256,64,16]{0,2,1:T(8,128)(2,1)S(1)}, u32[]{:S(2)}, u32[]{:S(2)}) async-start(bf16[256,64,16]{0,2,1:T(8,128)(2,1)} %bitcast.4), calls=%async_computation | async-start | bytes 1048576 | tf_op jit(solution)/shard_map/all_to_all | solution.py:85
  67.9 2.8 %gather_fusion = f32[1024,16]{1,0:T(8,128)S(1)} fusion(f32[32,16]{1,0:T(8,128)S(1)} %copy.112, s32[1024]{0:T(1024)S(1)} %broadcast_clamp_fusion), kind=kCustom, calls=%fused_computation | custom fusion | bytes 135168 | tf_op jit(solution)/shard_map/gather | solution.py:27
  70.8 0.9 copy.113
  73.5 5.2 %all-to-all-done = bf16[256,64,16]{0,2,1:T(8,128)(2,1)S(1)} async-done(((bf16[256,64,16]{0,2,1:T(8,128)(2,1)}), bf16[256,64,16]{0,2,1:T(8,128)(2,1)S(1)}, u32[]{:S(2)}, u32[]{:S(2)}) %all-to-all-start) | async-done | bytes 524320 | tf_op jit(solution)/shard_map/all_to_all | solution.py:85
  78.9 0.9 reshape.74
  79.8 1.7 convolution_bitcast_fusion
  81.5 11.7 %slice.199 = f32[256,16,16]{0,1,2:T(8,128)S(1)} slice(f32[512,16,16]{0,1,2:T(8,128)S(1)} %convolution_bitcast_fusion), slice={[0:511:2], [0:16:1], [0:16:1]} | slice | bytes 524288 | tf_op jit(solution)/shard_map/slice | solution.py:40
  93.2 11.7 %slice.200 = f32[256,16,16]{0,1,2:T(8,128)S(1)} slice(f32[512,16,16]{0,1,2:T(8,128)S(1)} %convolution_bitcast_fusion), slice={[1:512:2], [0:16:1], [0:16:1]} | slice | bytes 524288 | tf_op jit(solution)/shard_map/slice | solution.py:40
  105.0 4.5 %slice.204 = f32[128,16,16]{0,1,2:T(8,128)S(1)} slice(f32[256,16,16]{0,1,2:T(8,128)S(1)} %multiply_add_fusion), slice={[0:255:2], [0:16:1], [0:16:1]} | slice | bytes 262144 | tf_op jit(solution)/shard_map/slice | solution.py:40
  109.5 4.5 %slice.205 = f32[128,16,16]{0,1,2:T(8,128)S(1)} slice(f32[256,16,16]{0,1,2:T(8,128)S(1)} %multiply_add_fusion), slice={[1:256:2], [0:16:1], [0:16:1]} | slice | bytes 262144 | tf_op jit(solution)/shard_map/slice | solution.py:40
  114.8 2.8 %slice.209 = f32[64,16,16]{0,1,2:T(8,128)S(1)} slice(f32[128,16,16]{0,1,2:T(8,128)S(1)} %multiply_add_fusion.7), slice={[0:127:2], [0:16:1], [0:16:1]} | slice | bytes 131072 | tf_op jit(solution)/shard_map/slice | solution.py:40
  117.6 2.4 slice.210
  120.7 1.2 slice.214
  122.0 1.3 slice.215
  126.8 1.1 slice.225
  127.9 1.0 multiply_add_fusion.3
  128.9 0.9 slice.229
  129.8 0.9 slice.230
  130.7 1.1 multiply_add_fusion.2
  131.8 0.8 slice.234
  132.6 0.8 slice.235
  133.5 0.9 slice.242
  134.3 1.0 slice.244
  135.4 1.3 slice.246
  136.6 1.8 slice.248
  138.5 2.9 %slice.250 = f32[63,16,16]{0,1,2:T(8,128)} slice(f32[128,16,16]{0,1,2:T(8,128)S(1)} %multiply_add_fusion.7), slice={[2:128:2], [0:16:1], [0:16:1]} | slice | bytes 129024 | tf_op jit(solution)/shard_map/slice | solution.py:40
  141.4 5.9 %slice.252 = f32[127,16,16]{0,1,2:T(8,128)} slice(f32[256,16,16]{0,1,2:T(8,128)} %copy-done.1), slice={[2:256:2], [0:16:1], [0:16:1]} | slice | bytes 260096 | tf_op jit(solution)/shard_map/slice | solution.py:40
  147.3 12.1 %slice.254 = f32[255,16,16]{0,1,2:T(8,128)} slice(f32[512,16,16]{0,1,2:T(8,128)S(1)} %convolution_bitcast_fusion), slice={[2:512:2], [0:16:1], [0:16:1]} | slice | bytes 522240 | tf_op jit(solution)/shard_map/slice | solution.py:40
  159.4 1.1 multiply_add_fusion.1
  160.5 1.0 slice_add_fusion.1
  162.5 1.1 pad.58
  163.7 6.2 %pad.59 = f32[4,16,16]{0,1,2:T(8,128)S(1)} pad(f32[2,16,16]{0,1,2:T(8,128)} %pad_add_fusion, f32[]{:T(128)} %constant.12.clone.1), padding=1_0_1x0_0_0x0_0_0 | pad | bytes 6148 | tf_op jit(solution)/shard_map/pad | solution.py:40
  169.9 1.2 pad.61
  171.1 1.0 fusion.20
  172.3 1.2 pad.60
  173.5 0.8 fusion.19
  174.4 1.3 pad.62
  175.8 1.4 pad.63
  177.2 1.6 pad.65
  179.7 1.8 pad.64
  181.5 0.8 fusion.17
  182.5 2.1 pad.66
  184.6 2.2 pad.67
  186.8 3.2 %pad.69 = f32[128,16,16]{0,1,2:T(8,128)S(1)} pad(f32[64,16,16]{0,1,2:T(8,128)S(1)} %add.174, f32[]{:T(128)} %constant.12.clone.1), padding=1_0_1x0_0_0x0_0_0 | pad | bytes 196612 | tf_op jit(solution)/shard_map/pad | solution.py:40
  190.3 3.2 %pad.68 = f32[128,16,16]{0,1,2:T(8,128)S(1)} pad(f32[64,16,16]{0,1,2:T(8,128)S(1)} %pad_maximum_fusion.6, f32[]{:T(128)} %constant.12.clone.1), padding=0_1_1x0_0_0x0_0_0 | pad | bytes 196612 | tf_op jit(solution)/shard_map/pad | solution.py:40
  193.8 5.4 %pad.70 = f32[256,16,16]{0,1,2:T(8,128)S(1)} pad(f32[128,16,16]{0,1,2:T(8,128)S(1)} %pad_maximum_fusion.7, f32[]{:T(128)} %constant.12.clone.1), padding=0_1_1x0_0_0x0_0_0 | pad | bytes 393220 | tf_op jit(solution)/shard_map/pad | solution.py:40
  199.1 5.4 %pad.71 = f32[256,16,16]{0,1,2:T(8,128)S(1)} pad(f32[128,16,16]{0,1,2:T(8,128)S(1)} %add.176, f32[]{:T(128)} %constant.12.clone.1), padding=1_0_1x0_0_0x0_0_0 | pad | bytes 393220 | tf_op jit(solution)/shard_map/pad | solution.py:40
  204.6 9.7 %pad.118 = f32[512,16,16]{0,1,2:T(8,128)S(1)} pad(f32[256,16,16]{0,1,2:T(8,128)S(1)} %add.178, f32[]{:T(128)} %constant.12.clone.1), padding=1_0_1x0_0_0x0_0_0 | pad | bytes 786436
  214.2 1.1 fusion.9
  215.5 9.7 %pad.94 = f32[511,16,16]{0,1,2:T(8,128)S(1)} pad(f32[256,16,16]{0,1,2:T(8,128)S(1)} %pad_maximum_fusion, f32[]{:T(128)} %constant.12.clone.1), padding=0_0_1x0_0_0x0_0_0 | pad | bytes 785412 | tf_op jit(solution)/shard_map/slice | solution.py:47
  225.3 3.1 %fusion.13 = f32[16,512,32]{1,2,0:T(8,128)S(1)} fusion(bf16[512,32,16]{1,0,2:T(8,128)(2,1)S(1)} %reshape.74, f32[32,32,16]{1,0,2:T(8,128)} %copy.113, pred[32,32]{1,0:T(8,128)(4,1)S(1)} %copy-done.15), kind=kOutput, calls=%fused_computation.25 | convolution fusion | flops 100679680 | bytes 1639424 | tf_op jit(solution)/shard_map/ijc,bjc->bic/dot_general | solution.py:37
  228.4 1.4 fusion.2
  229.8 2.6 copy.135
  232.4 3.3 %all_to_all.29 = f32[64,256,16]{1,0,2:T(8,128)S(1)} reshape(f32[512,32,16]{1,0,2:T(8,128)} %copy.135) | data formatting | bytes 2097152 | tf_op jit(solution)/shard_map/all_to_all | solution.py:95
  235.8 1.6 copy.136
  237.4 6.2 %all-to-all-start.1 = ((f32[64,256,16]{1,2,0:T(8,128)}), f32[64,256,16]{1,2,0:T(8,128)S(1)}, u32[]{:S(2)}, u32[]{:S(2)}) async-start(f32[64,256,16]{1,2,0:T(8,128)} %copy.136), calls=%async_computation.1 | async-start | bytes 2097152 | tf_op jit(solution)/shard_map/all_to_all | solution.py:95
  243.8 28.3 %all-to-all-done.1 = f32[64,256,16]{1,2,0:T(8,128)S(1)} async-done(((f32[64,256,16]{1,2,0:T(8,128)}), f32[64,256,16]{1,2,0:T(8,128)S(1)}, u32[]{:S(2)}, u32[]{:S(2)}) %all-to-all-start.1) | async-done | bytes 1048608 | tf_op jit(solution)/shard_map/all_to_all | solution.py:95
  272.3 1.0 copy.137
  (110 shorter events, 19.9 us)
Async XLA Ops:
  0.0 6.1 %copy-start.16 = (bf16[64,128]{1,0:T(8,128)(2,1)S(1)}, bf16[64,128]{1,0:T(8,128)(2,1)}, u32[]{:S(2)}) copy-start(bf16[64,128]{1,0:T(8,128)(2,1)} %param.12) | copy-start | bytes 49156
  1.5 9.1 %collective-permute-start = (bf16[127,1024]{1,0:T(8,128)(2,1)S(1)}, bf16[127,1024]{1,0:T(8,128)(2,1)S(1)}, u32[]{:S(2)}, u32[]{:S(2)}) collective-permute-start(bf16[127,1024]{1,0:T(8,128)(2,1)S(1)} %slice.258), channel_id=1, source_target_pairs={{0,8},{8,16},{16,24},{24,32},{32,40},{40,48},{48,56},{56,64},{64,7... | collective-permute-start | bytes 780296 | tf_op jit(solution)/shard_map/ppermute | solution.py:12
  10.8 14.1 %copy-start.2 = (bf16[256,1024]{1,0:T(8,128)(2,1)S(1)}, bf16[256,1024]{1,0:T(8,128)(2,1)}, u32[]{:S(2)}) copy-start(bf16[256,1024]{1,0:T(8,128)(2,1)} %param.9) | copy-start | bytes 1572868
  10.8 32.6 %copy-start.3 = (bf16[256,1024]{1,0:T(8,128)(2,1)S(1)}, bf16[256,1024]{1,0:T(8,128)(2,1)}, u32[]{:S(2)}) copy-start(bf16[256,1024]{1,0:T(8,128)(2,1)} %param.15) | copy-start | bytes 1572868
  10.8 32.6 %copy-start.18 = (f32[1024]{0:T(1024)S(1)}, f32[1024]{0:T(1024)}, u32[]{:S(2)}) copy-start(f32[1024]{0:T(1024)} %param.13) | copy-start | bytes 12292
  44.7 34.0 %all-to-all-start = ((bf16[256,64,16]{0,2,1:T(8,128)(2,1)}), bf16[256,64,16]{0,2,1:T(8,128)(2,1)S(1)}, u32[]{:S(2)}, u32[]{:S(2)}) async-start(bf16[256,64,16]{0,2,1:T(8,128)(2,1)} %bitcast.4), calls=%async_computation | async-start | bytes 1048576 | tf_op jit(solution)/shard_map/all_to_all | solution.py:85
  61.4 0.5 copy-start.19
  61.6 6.4 %copy-start.10 = (f32[16,16]{0,1:T(8,128)}, f32[16,16]{0,1:T(8,128)S(1)}, u32[]{:S(2)}) copy-start(f32[16,16]{0,1:T(8,128)S(1)} %copy.110) | copy-start | bytes 3076
  81.5 77.9 %copy-start = (f32[512,16,16]{0,1,2:T(8,128)}, f32[512,16,16]{0,1,2:T(8,128)S(1)}, u32[]{:S(2)}) copy-start(f32[512,16,16]{0,1,2:T(8,128)S(1)} %convolution_bitcast_fusion) | copy-start | bytes 1572868
  105.0 4.5 %copy-start.1 = (f32[256,16,16]{0,1,2:T(8,128)}, f32[256,16,16]{0,1,2:T(8,128)S(1)}, u32[]{:S(2)}) copy-start(f32[256,16,16]{0,1,2:T(8,128)S(1)} %multiply_add_fusion) | copy-start | bytes 786436
  162.4 11.1 %copy-start.9 = (f32[7,16,16]{0,1,2:T(8,128)S(1)}, f32[7,16,16]{0,1,2:T(8,128)}, u32[]{:S(2)}) copy-start(f32[7,16,16]{0,1,2:T(8,128)} %slice.244) | copy-start | bytes 21508
  169.9 8.9 %copy-start.8 = (f32[15,16,16]{0,1,2:T(8,128)S(1)}, f32[15,16,16]{0,1,2:T(8,128)}, u32[]{:S(2)}) copy-start(f32[15,16,16]{0,1,2:T(8,128)} %slice.246) | copy-start | bytes 46084
  173.4 8.1 %copy-start.7 = (f32[31,16,16]{0,1,2:T(8,128)S(1)}, f32[31,16,16]{0,1,2:T(8,128)}, u32[]{:S(2)}) copy-start(f32[31,16,16]{0,1,2:T(8,128)} %slice.248) | copy-start | bytes 95236
  177.1 12.9 %copy-start.6 = (f32[63,16,16]{0,1,2:T(8,128)S(1)}, f32[63,16,16]{0,1,2:T(8,128)}, u32[]{:S(2)}) copy-start(f32[63,16,16]{0,1,2:T(8,128)} %slice.250) | copy-start | bytes 193540
  177.1 12.9 %copy-start.13 = (f32[16,16]{0,1:T(8,128)S(1)}, f32[16,16]{0,1:T(8,128)}, u32[]{:S(2)}) copy-start(f32[16,16]{0,1:T(8,128)} %copy.120) | copy-start | bytes 3076
  181.5 12.0 %copy-start.5 = (f32[127,16,16]{0,1,2:T(8,128)S(1)}, f32[127,16,16]{0,1,2:T(8,128)}, u32[]{:S(2)}) copy-start(f32[127,16,16]{0,1,2:T(8,128)} %slice.252) | copy-start | bytes 390148
  181.5 12.0 %copy-start.12 = (f32[16,16]{0,1:T(8,128)S(1)}, f32[16,16]{0,1:T(8,128)}, u32[]{:S(2)}) copy-start(f32[16,16]{0,1:T(8,128)} %copy.118) | copy-start | bytes 3076
  181.5 12.1 %slice-start.1 = ((f32[256,16,16]{0,1,2:T(8,128)}), f32[1,16,16]{0,1,2:T(8,128)S(1)}, s32[]{:S(2)}) async-start(f32[256,16,16]{0,1,2:T(8,128)} %copy-done.1), calls=%async_computation.3 | async-start | bytes 262144 | tf_op jit(solution)/shard_map/slice | solution.py:40
  193.5 21.8 %slice-start = ((f32[512,16,16]{0,1,2:T(8,128)}), f32[1,16,16]{0,1,2:T(8,128)S(1)}, s32[]{:S(2)}) async-start(f32[512,16,16]{0,1,2:T(8,128)} %copy-done), calls=%async_computation.2 | async-start | bytes 262144 | tf_op jit(solution)/shard_map/slice | solution.py:40
  215.3 9.9 %copy-start.15 = (pred[32,32]{1,0:T(8,128)(4,1)S(1)}, pred[32,32]{1,0:T(8,128)(4,1)}, u32[]{:S(2)}) copy-start(pred[32,32]{1,0:T(8,128)(4,1)} %subtract_compare_fusion) | copy-start | bytes 3076
  225.2 3.2 %copy-start.11 = (f32[16,16]{0,1:T(8,128)S(1)}, f32[16,16]{0,1:T(8,128)}, u32[]{:S(2)}) copy-start(f32[16,16]{0,1:T(8,128)} %copy-done.10) | copy-start | bytes 3076
  225.2 3.2 %copy-start.14 = (f32[16,16]{0,1:T(8,128)S(1)}, f32[16,16]{0,1:T(8,128)}, u32[]{:S(2)}) copy-start(f32[16,16]{0,1:T(8,128)} %copy.134) | copy-start | bytes 3076
  225.3 3.2 %copy-start.17 = (f32[512]{0:T(512)S(1)}, f32[512]{0:T(512)}, u32[]{:S(2)}) copy-start(f32[512]{0:T(512)} %convert_multiply_fusion) | copy-start | bytes 6148
  225.3 3.2 %copy-start.20 = (f32[32]{0:T(128)S(1)}, f32[32]{0:T(128)}, u32[]{:S(2)}) copy-start(f32[32]{0:T(128)} %copy-done.19) | copy-start | bytes 388
  235.8 7.8 %copy-start.4 = (bf16[256,1024]{1,0:T(8,128)(2,1)S(1)}, bf16[256,1024]{1,0:T(8,128)(2,1)}, u32[]{:S(2)}) copy-start(bf16[256,1024]{1,0:T(8,128)(2,1)} %param.14) | copy-start | bytes 1572868
  237.4 34.7 %all-to-all-start.1 = ((f32[64,256,16]{1,2,0:T(8,128)}), f32[64,256,16]{1,2,0:T(8,128)S(1)}, u32[]{:S(2)}, u32[]{:S(2)}) async-start(f32[64,256,16]{1,2,0:T(8,128)} %copy.136), calls=%async_computation.1 | async-start | bytes 2097152 | tf_op jit(solution)/shard_map/all_to_all | solution.py:95
where the time goes:
time: 278 us; the launch traced here: 273 us
  local copies, waits for them, and re-layouts  152 us (55%)
  waiting for transfers between devices  35.9 us (13%)
  starting transfers between devices  27.5 us (10%)
  matrix products  20.3 us (7%)
  other arithmetic  18.5 us (7%)
  blocking collectives  18.2 us (7%)
    slice x29, local copies, waits for them, and re-layouts, local_pass(): _, states = lax.associative_scan(join_states, (decays, closing), axis=0)  73.4 us
    pad x14, local copies, waits for them, and re-layouts, local_pass(): _, states = lax.associative_scan(join_states, (decays, closing), axis=0)  37.3 us
    all_to_all x1, waiting for transfers between devices, on_device(): lax.all_to_all(result.reshape(full_len, per_device), 'ctx', split_axis=0,...  28.3 us
    psum x1, blocking collectives, on_device(): squares = lax.psum(jnp.sum(z_one * z_one, axis=1), 'tp')  18.2 us
    all_to_all x1, starting transfers between devices, on_device(): lax.all_to_all(u_two, 'ctx', split_axis=1, concat_axis=0, tiled=True)  16.7 us
    conv_general_dilated x1, matrix products, short_conv(): lax.conv_general_dilated(extended[None], kernel, (1,), 'VALID', dimension...  14.1 us
    add x16, other arithmetic, join_states(): return (earlier[0] * later[0], later[0] * earlier[1] + later[1])  12.2 us
    unnamed x44, local copies, waits for them, and re-layouts  10.2 us
  transfers between devices with their start and end apart: 3, of which 3 were waited for; matrix products, arithmetic and copies ran while one was open for 5% of the time, Pallas kernels for 0%

commit v1 on v0

v1 whole, which is shorter than its diff:
```python
import functools

import jax
import jax.numpy as jnp
from jax import lax
from jax.experimental import pallas as pl
from jax.experimental.pallas import tpu as pltpu
from jax.sharding import PartitionSpec as P

LANES = 128
ROWS = 8
UNROLL = 8
F32 = jnp.float32
BF16 = jnp.bfloat16
INTERPRET = False


def in_vmem(count):
    return [pl.BlockSpec(memory_space=pltpu.VMEM)] * count


def call(kernel, out_shape, args, scratch=(), smem=0, name=None):
    specs = [pl.BlockSpec(memory_space=pltpu.SMEM)] * smem + in_vmem(len(args) - smem)
    outs = in_vmem(len(out_shape)) if isinstance(out_shape, (list, tuple)) else in_vmem(1)[0]
    return pl.pallas_call(
        kernel,
        out_shape=out_shape,
        in_specs=specs,
        out_specs=outs,
        scratch_shapes=list(scratch),
        name=name,
        interpret=INTERPRET,
    )(*args)


def shape(dims, kind=F32):
    return jax.ShapeDtypeStruct(dims, kind)


def channel_rows(ref, table):
    modes = table.shape[0]
    for block in range(table.shape[1] // LANES):
        piece = table[:, block * LANES : (block + 1) * LANES]
        ref[pl.ds(block, modes, stride=ROWS), :] = piece


def tables_kernel(span, filter_ref, rates_ref, weights_ref, tap_ref, step_ref, weight_ref, decay_ref):
    groups, taps = filter_ref.shape
    row = lax.broadcasted_iota(jnp.int32, (taps, taps), 0)
    col = lax.broadcasted_iota(jnp.int32, (taps, taps), 1)
    flip = jnp.where(((row + col) & (taps - 1)) == 0, 1.0, 0.0).astype(BF16)
    mirrored = jnp.dot(filter_ref[...], flip, preferred_element_type=F32)
    before = col > row
    for group in range(groups):
        line = jnp.broadcast_to(mirrored[group : group + 1, :], (taps, taps))
        circulant = pltpu.roll(line, 0, axis=1, stride=1, stride_axis=0)
        tap_ref[group, :, :taps] = jnp.where(before, circulant, 0.0).astype(BF16)
        tap_ref[group, :, taps:] = jnp.where(before, 0.0, circulant).astype(BF16)
    rates = rates_ref[...]
    channel_rows(step_ref, jnp.exp(-rates))
    channel_rows(decay_ref, jnp.exp(-rates * span))
    channel_rows(weight_ref, weights_ref[...])


def conv_kernel(
    group_ch, k_ref, v_ref, q_ref, gate_ref, gain_ref, halo_ref, tap_ref, value_ref, square_ref
):
    length, channels = k_ref.shape
    half = length // 2
    lane = lax.broadcasted_iota(jnp.int32, (half, 2 * LANES), 1)
    member = (lane & (LANES - 1)) // group_ch
    per_tile = LANES // group_ch
    partial = [jnp.zeros((half, LANES), F32), jnp.zeros((half, LANES), F32)]
    for tile in range(channels // LANES):
        cols = slice(tile * LANES, (tile + 1) * LANES)
        u_one = (k_ref[:, cols].astype(F32) * v_ref[:, cols].astype(F32)).astype(BF16)
        early = jnp.concatenate([halo_ref[:, cols], u_one[:half]], axis=0)
        windows = jnp.concatenate([early, u_one], axis=1)
        conv = jnp.zeros((half, 2 * LANES), F32)
        for place in range(per_tile):
            product = jnp.dot(
                tap_ref[tile * per_tile + place], windows, preferred_element_type=F32
            )
            conv = jnp.where(member == place, product, conv)
        for part in range(2):
            rows = slice(part * half, (part + 1) * half)
            z_one = q_ref[rows, cols].astype(F32) * conv[:, part * LANES : (part + 1) * LANES]
            partial[part] = partial[part] + z_one * z_one
            value = gate_ref[rows, cols].astype(F32) * (z_one * gain_ref[:, cols])
            value_ref[pl.ds(part * half * ROWS + tile, half, stride=ROWS), :] = value
    for part in range(2):
        line = jnp.sum(partial[part].T, axis=0, keepdims=True)
        for copy in range(square_ref.shape[0]):
            square_ref[copy, part : part + 1, :] = line


def state_kernel(width, square_ref, value_ref, step_ref, u_ref, state_ref, scale_ref):
    half = LANES
    total = square_ref[0]
    for peer in range(1, square_ref.shape[0]):
        total = total + square_ref[peer]
    scale = lax.rsqrt(total / width + 1e-06)
    for part in range(2):
        line = jnp.broadcast_to(scale[part : part + 1, :], (half, LANES))
        scale_ref[part * half : (part + 1) * half, :] = line.T
    modes = step_ref.shape[0] // ROWS
    steps = [step_ref[m * ROWS : (m + 1) * ROWS, :] for m in range(modes)]

    def token(t, states):
        at = pl.ds(pl.multiple_of(t * ROWS, ROWS), ROWS)
        factor = jnp.broadcast_to(scale_ref[pl.ds(t, 1), :], (ROWS, LANES))
        u_two = (value_ref[at, :] * factor).astype(BF16).astype(F32)
        u_ref[at, :] = u_two
        return tuple(a * s + u_two for a, s in zip(steps, states))

    zero = tuple(jnp.zeros((ROWS, LANES), F32) for _ in range(modes))
    states = lax.fori_loop(0, 2 * half, token, zero, unroll=UNROLL)
    for m in range(modes):
        state_ref[m * ROWS : (m + 1) * ROWS, :] = states[m]


def scan_kernel(place_ref, state_ref, decay_ref, entry_ref):
    decay = decay_ref[place_ref[0]]
    entry = jnp.zeros_like(decay)
    for device in range(state_ref.shape[0]):
        entry_ref[device] = entry
        entry = decay * entry + state_ref[device]


def output_kernel(entry_ref, u_ref, step_ref, weight_ref, gate_ref, out_ref, conv_ref):
    modes = step_ref.shape[0] // ROWS
    rows_of = lambda ref: [ref[m * ROWS : (m + 1) * ROWS, :] for m in range(modes)]
    steps, weights = rows_of(step_ref), rows_of(weight_ref)
    length, channels = gate_ref.shape

    def token(t, states):
        at = pl.ds(pl.multiple_of(t * ROWS, ROWS), ROWS)
        u_two = u_ref[at, :]
        states = tuple(a * s + u_two for a, s in zip(steps, states))
        terms = [w * s for w, s in zip(weights, states)]
        while len(terms) > 1:
            terms = [x + y for x, y in zip(terms[::2], terms[1::2])]
        conv_ref[at, :] = terms[0]
        return states

    lax.fori_loop(0, length, token, tuple(rows_of(entry_ref)), unroll=UNROLL)
    for tile in range(channels // LANES):
        cols = slice(tile * LANES, (tile + 1) * LANES)
        conv_two = conv_ref[pl.ds(tile, length, stride=ROWS), :]
        out_ref[:, cols] = (gate_ref[:, cols].astype(F32) * conv_two).astype(BF16)


def on_device(q_one, k_one, v_one, mr_filter, norm_gain, q_two, k_two, li_rates, li_residues):
    length, channels = q_one.shape
    groups, taps = mr_filter.shape
    modes = li_rates.shape[0]
    devices, peers = lax.axis_size("ctx"), lax.axis_size("tp")
    width = channels * peers
    flat = (modes * ROWS, LANES)

    tail = (k_one[length - taps :].astype(F32) * v_one[length - taps :].astype(F32)).astype(BF16)
    halo = lax.ppermute(tail, "ctx", [(i, i + 1) for i in range(devices - 1)])

    weights = li_residues * jnp.sqrt(-jnp.expm1(-2.0 * li_rates))
    tap_table, steps, mode_weights, decays = call(
        functools.partial(tables_kernel, float(length)),
        [shape((groups, taps, 2 * taps), BF16), shape(flat), shape(flat), shape(flat)],
        (mr_filter, li_rates, weights),
        name="tables",
    )
    value, squares = call(
        functools.partial(conv_kernel, channels // groups),
        [shape((length * ROWS, LANES)), shape((peers, 2, LANES))],
        (k_one, v_one, q_one, k_two, norm_gain[None, :], halo, tap_table),
        name="conv",
    )
    squares = lax.all_to_all(squares, "tp", split_axis=0, concat_axis=0, tiled=True)
    u_two, states = call(
        functools.partial(state_kernel, float(width)),
        [shape((length * ROWS, LANES)), shape(flat)],
        (squares, value, steps),
        scratch=[pltpu.VMEM((length, LANES), F32)],
        name="states",
    )
    shares = (devices, flat[0] // devices, LANES)
    received = lax.all_to_all(
        states.reshape(shares), "ctx", split_axis=0, concat_axis=0, tiled=True
    )
    place = lax.axis_index("ctx").astype(jnp.int32).reshape(1)
    entries = call(
        scan_kernel,
        shape(shares),
        (place, received, decays.reshape(shares)),
        smem=1,
        name="scan",
    )
    entries = lax.all_to_all(entries, "ctx", split_axis=0, concat_axis=0, tiled=True)
    return call(
        output_kernel,
        shape((length, channels), BF16),
        (entries.reshape(flat), u_two, steps, mode_weights, q_two),
        scratch=[pltpu.VMEM((length * ROWS, LANES), F32)],
        name="output",
    )


def solution(mesh):
    in_specs = (
        P("ctx", "tp"),
        P("ctx", "tp"),
        P("ctx", "tp"),
        P("tp", None),
        P("tp"),
        P("ctx", "tp"),
        P("ctx", "tp"),
        P(None, "tp"),
        P(None, "tp"),
    )
    return jax.shard_map(
        on_device, mesh=mesh, in_specs=in_specs, out_specs=P("ctx", "tp"), check_vma=False
    )
```

time: 278 us -> 81.9 us (0.29); the launches traced: 273 us -> 81.4 us
  local copies, waits for them, and re-layouts: 152 us -> 1.33 us
  waiting for transfers between devices: 35.9 us -> 9.77 us
  matrix products: 20.3 us -> 0 us
  Pallas kernels: 0 us -> 19.3 us
  other arithmetic: 18.5 us -> 2.64 us
  blocking collectives: 18.2 us -> 31.8 us
  starting transfers between devices: 27.5 us -> 16.6 us
    slice x31 -> x0, local copies, waits for them, and re-layouts: 83.2 us -> none  [the longest x29 73.4 us: local_pass(): _, states = lax.associative_scan(join_states, (decays, closing), axis=0)]
    pad x14 -> x0, local copies, waits for them, and re-layouts: 37.3 us -> none  [local_pass(): _, states = lax.associative_scan(join_states, (decays, closing), axis=0)]
    all_to_all x0 -> x2, blocking collectives: none -> 31.8 us  [the longest x1 16.7 us: on_device(): lax.all_to_all(squares, 'tp', split_axis=0, concat_axis=0, tiled=True)]
    all_to_all x2 -> x1, waiting for transfers between devices: 33.5 us -> 9.77 us  [on_device(): lax.all_to_all(states.reshape(shares), 'ctx', split_axis=0, concat_axis=0...]
    pallas_call x0 -> x5, Pallas kernels: none -> 19.3 us  [call(): pl.pallas_call(kernel, out_shape=out_shape, in_specs=specs, out_specs=out...]
    psum x1 -> x0, blocking collectives: 18.2 us -> none  [on_device(): squares = lax.psum(jnp.sum(z_one * z_one, axis=1), 'tp')]
    conv_general_dilated x1 -> x0, matrix products: 14.1 us -> none  [short_conv(): lax.conv_general_dilated(extended[None], kernel, (1,), 'VALID', dimension...]
    add x25 -> x0, other arithmetic: 13.1 us -> none  [the longest x16 12.2 us: join_states(): return (earlier[0] * later[0], later[0] * earlier[1] + later[1])]
  transfers between devices with their start and end apart: 3 -> 2, of which waited for: 3 -> 1; matrix products, arithmetic and copies ran while one was open for 5% -> 2% of each run, Pallas kernels for 0% -> 5%
where the time goes in v1:
time: 81.9 us; the launch traced here: 81.4 us
  blocking collectives  31.8 us (39%)
  Pallas kernels  19.3 us (24%)
  starting transfers between devices  16.6 us (20%)
  waiting for transfers between devices  9.77 us (12%)
  other arithmetic  2.64 us (3%)
  local copies, waits for them, and re-layouts  1.33 us (2%)
    pallas_call x5, Pallas kernels, call(): pl.pallas_call(kernel, out_shape=out_shape, in_specs=specs, out_specs=out...  19.3 us
    all_to_all x1, blocking collectives, on_device(): lax.all_to_all(squares, 'tp', split_axis=0, concat_axis=0, tiled=True)  16.7 us
    all_to_all x1, blocking collectives, on_device(): lax.all_to_all(entries, 'ctx', split_axis=0, concat_axis=0, tiled=True)  15.1 us
    all_to_all x1, starting transfers between devices, on_device(): lax.all_to_all(states.reshape(shares), 'ctx', split_axis=0, concat_axis=0...  12 us
    all_to_all x1, waiting for transfers between devices, on_device(): lax.all_to_all(states.reshape(shares), 'ctx', split_axis=0, concat_axis=0...  9.77 us
    ppermute x1, starting transfers between devices, on_device(): halo = lax.ppermute(tail, 'ctx', [(i, i + 1) for i in range(devices - 1)])  4.58 us
  transfers between devices with their start and end apart: 2, of which 1 were waited for; matrix products, arithmetic and copies ran while one was open for 2% of the time, Pallas kernels for 5%

profile of v1, /device:TPU:1, one launch (start us, length us, event | category | flops | bytes accessed | tf_op | source)
XLA Modules:
  0.0 81.4 jit_solution(2664293588659918999)
XLA Ops:
  0.0 1.1 %multiply_convert_fusion = bf16[128,1024]{1,0:T(8,128)(2,1)S(1)} fusion(bf16[256,1024]{1,0:T(8,128)(2,1)} %v_ref.1, bf16[256,1024]{1,0:T(8,128)(2,1)} %k_ref.1), kind=kLoop, calls=%fused_computation | loop fusion | flops 524288 | bytes 786432 | tf_op jit(solution)/shard_map/convert_element_type | solution.py:161
  1.1 4.6 %collective-permute-start = (bf16[128,1024]{1,0:T(8,128)(2,1)S(1)}, bf16[128,1024]{1,0:T(8,128)(2,1)S(1)}, u32[]{:S(2)}, u32[]{:S(2)}) collective-permute-start(bf16[128,1024]{1,0:T(8,128)(2,1)S(1)} %multiply_convert_fusion), channel_id=1, source_target_pairs={{0,8},{8,16},{16,24},{24,32},{32,40},{40,48},{48,56},{56,64},{64,7... | collective-permute-start | bytes 786440 | tf_op jit(solution)/shard_map/ppermute | solution.py:162
  5.7 1.6 %sqrt_multiply_fusion.weights_ref = f32[16,1024]{1,0:T(8,128)} fusion(f32[16,1024]{1,0:T(8,128)} %param.17, f32[16,1024]{1,0:T(8,128)} %rates_ref.1), kind=kLoop, calls=%fused_computation.1 | loop fusion | flops 49152 | bytes 196608 | tf_op jit(solution)/shard_map/mul | solution.py:164
  7.2 3.8 %tables.1 = (bf16[64,128,256]{2,1,0:T(8,128)(2,1)}, f32[128,128]{1,0:T(8,128)}, f32[128,128]{1,0:T(8,128)}, f32[128,128]{1,0:T(8,128)}) custom-call(bf16[64,128]{1,0:T(8,128)(2,1)} %filter_ref.1, f32[16,1024]{1,0:T(8,128)} %rates_ref.1, f32[16,1024]{1,0:T(8,128)} %sqrt_multiply_fusion.weights_ref), custom_call_target="tpu_custom_call" | custom-call | tf_op jit(solution)/shard_map/tables/pallas_call | solution.py:25
  11.1 0.0 collective-permute-done.halo_ref
  11.1 0.0 copy-start
  11.1 0.7 copy-done
  11.8 5.4 %conv.1 = (f32[2048,128]{1,0:T(8,128)}, f32[8,2,128]{2,1,0:T(2,128)}) custom-call(bf16[256,1024]{1,0:T(8,128)(2,1)} %k_ref.1, bf16[256,1024]{1,0:T(8,128)(2,1)} %v_ref.1, bf16[256,1024]{1,0:T(8,128)(2,1)} %q_ref.1, bf16[256,1024]{1,0:T(8,128)(2,1)} %gate_ref.2, f32[1,1024]{1,0:T(1,128)} %bitcast.8, bf16[128,1024]{1,0:T(8,128)(2,1)} %copy-done, ...), custom_call_target="tpu_custom_call" | custom-call | tf_op jit(solution)/shard_map/conv/pallas_call | solution.py:25
  17.2 16.7 %all_to_all.15.square_ref = f32[8,2,128]{2,1,0:T(2,128)} all-to-all(f32[8,2,128]{2,1,0:T(2,128)} %get-tuple-element.14), channel_id=1, replica_groups=mesh['ctx'=64,'tp'=8] {'tp'}, dimensions={0} | all-to-all | bytes 16384 | tf_op jit(solution)/shard_map/all_to_all | solution.py:177
  33.9 3.7 %states.1 = (f32[2048,128]{1,0:T(8,128)}, f32[128,128]{1,0:T(8,128)}) custom-call(f32[8,2,128]{2,1,0:T(2,128)} %all_to_all.15.square_ref, f32[2048,128]{1,0:T(8,128)} %get-tuple-element.15.value_ref, f32[128,128]{1,0:T(8,128)} %get-tuple-element.16.step_ref), custom_call_target="tpu_custom_call" | custom-call | tf_op jit(solution)/shard_map/states/pallas_call | solution.py:25
  37.5 12.0 %all-to-all-start.1 = ((f32[64,2,128]{2,1,0:T(2,128)}), f32[64,2,128]{2,1,0:T(2,128)S(1)}, u32[]{:S(2)}, u32[]{:S(2)}) async-start(f32[64,2,128]{2,1,0:T(2,128)} %bitcast.7), calls=%async_computation.1 | async-start | bytes 131072 | tf_op jit(solution)/shard_map/all_to_all | solution.py:186
  49.5 9.8 %all-to-all-done.1.state_ref = f32[64,2,128]{2,1,0:T(2,128)S(1)} async-done(((f32[64,2,128]{2,1,0:T(2,128)}), f32[64,2,128]{2,1,0:T(2,128)S(1)}, u32[]{:S(2)}, u32[]{:S(2)}) %all-to-all-start.1) | async-done | bytes 65568 | tf_op jit(solution)/shard_map/all_to_all | solution.py:186
  59.3 0.0 copy-start.1
  59.3 0.6 copy-done.1
  59.9 1.6 %scan.1 = f32[64,2,128]{2,1,0:T(2,128)} custom-call(s32[1]{0:T(128)} %bitcast.place_ref, f32[64,2,128]{2,1,0:T(2,128)} %copy-done.1, f32[64,2,128]{2,1,0:T(2,128)} %bitcast.6), custom_call_target="tpu_custom_call" | custom-call | tf_op jit(solution)/shard_map/scan/pallas_call | solution.py:25
  61.6 15.1 %all_to_all.16 = f32[64,2,128]{2,1,0:T(2,128)} all-to-all(f32[64,2,128]{2,1,0:T(2,128)} %scan.1), channel_id=1, replica_groups=mesh['ctx'=64,'tp'=8] {'ctx'}, dimensions={0} | all-to-all | bytes 131072 | tf_op jit(solution)/shard_map/all_to_all | solution.py:197
  76.6 4.8 %output.1 = bf16[256,1024]{1,0:T(8,128)(2,1)} custom-call(f32[128,128]{1,0:T(8,128)} %bitcast.5, f32[2048,128]{1,0:T(8,128)} %get-tuple-element.19.u_ref, f32[128,128]{1,0:T(8,128)} %get-tuple-element.16.step_ref, f32[128,128]{1,0:T(8,128)} %get-tuple-element.20.weight_ref, bf16[256,1024]{1,0:T(8,128)(2,1)} %gate_ref.3), custom_call_target="tpu_custom_call" | custom-call | tf_op jit(solution)/shard_map/output/pallas_call | solution.py:25
Async XLA Ops:
  1.1 10.0 %collective-permute-start = (bf16[128,1024]{1,0:T(8,128)(2,1)S(1)}, bf16[128,1024]{1,0:T(8,128)(2,1)S(1)}, u32[]{:S(2)}, u32[]{:S(2)}) collective-permute-start(bf16[128,1024]{1,0:T(8,128)(2,1)S(1)} %multiply_convert_fusion), channel_id=1, source_target_pairs={{0,8},{8,16},{16,24},{24,32},{32,40},{40,48},{48,56},{56,64},{64,7... | collective-permute-start | bytes 786440 | tf_op jit(solution)/shard_map/ppermute | solution.py:162
  11.1 0.7 copy-start
  37.5 21.8 %all-to-all-start.1 = ((f32[64,2,128]{2,1,0:T(2,128)}), f32[64,2,128]{2,1,0:T(2,128)S(1)}, u32[]{:S(2)}, u32[]{:S(2)}) async-start(f32[64,2,128]{2,1,0:T(2,128)} %bitcast.7), calls=%async_computation.1 | async-start | bytes 131072 | tf_op jit(solution)/shard_map/all_to_all | solution.py:186
  59.3 0.6 copy-start.1

commit v2 on v1

v2 whole, which is shorter than its diff:
```python
import functools

import jax
import jax.numpy as jnp
from jax import lax
from jax.experimental import pallas as pl
from jax.experimental.pallas import tpu as pltpu
from jax.sharding import PartitionSpec as P

LANES = 128
ROWS = 8
BLOCK = 64
UNROLL = 8
CHUNK = 16
QUARTERS = 4
F32 = jnp.float32
BF16 = jnp.bfloat16
INTERPRET = False
IN_VMEM = pl.BlockSpec(memory_space=pltpu.VMEM)
IN_SMEM = pl.BlockSpec(memory_space=pltpu.SMEM)
IN_HBM = pl.BlockSpec(memory_space=pltpu.HBM)


def hbm(array):
    return array if INTERPRET else pltpu.with_memory_space_constraint(array, pltpu.HBM)


def call(name, kernel, inputs, outputs, scratch=()):
    return pl.pallas_call(
        kernel,
        out_shape=[jax.ShapeDtypeStruct(dims, kind) for _, dims, kind in outputs],
        in_specs=[spec for spec, _ in inputs],
        out_specs=[spec for spec, _, _ in outputs],
        scratch_shapes=list(scratch),
        compiler_params=pltpu.CompilerParams(vmem_limit_bytes=16 * 2**20),
        interpret=INTERPRET,
        name=name,
    )(*[hbm(array) if spec is IN_HBM else array for spec, array in inputs])


def fetch(pairs, sems):
    copies = [
        pltpu.make_async_copy(source, target, sems.at[i])
        for i, (source, target) in enumerate(pairs)
    ]
    for copy in copies:
        copy.start()
    return copies


def channel_rows(ref, table):
    modes = table.shape[0]
    for block in range(table.shape[1] // LANES):
        piece = table[:, block * LANES : (block + 1) * LANES]
        ref[pl.ds(block, modes, stride=ROWS), :] = piece


def one_minus_exp(x):
    total = jnp.full_like(x, 1.0)
    for order in range(11, 1, -1):
        total = 1.0 - total * x * (1.0 / order)
    return jnp.where(x < 0.5, x * total, 1.0 - jnp.exp(-x))


def product_bf16(left, right):
    return (left.astype(F32) * right.astype(F32)).astype(BF16)


def filtered(tap_ref, tile, per_tile, windows, member):
    conv = None
    for place in range(per_tile):
        product = jnp.dot(tap_ref[tile * per_tile + place], windows, preferred_element_type=F32)
        conv = product if place == 0 else jnp.where(member == place, product, conv)
    return conv


def gated(conv, tile, q, gate, gain, partial, value_ref):
    for part in range(2):
        rows = slice(part * BLOCK, (part + 1) * BLOCK)
        z_one = q[rows].astype(F32) * conv[:, part * LANES : (part + 1) * LANES]
        partial[part] = partial[part] + z_one * z_one
        value = gate[rows].astype(F32) * (z_one * gain)
        value_ref[pl.ds(part * BLOCK * ROWS + tile, BLOCK, stride=ROWS), :] = value


def token_row(partial):
    return jnp.sum(jnp.concatenate(partial, axis=0).T, axis=0, keepdims=True)


def lane_member(group_ch):
    lane = lax.broadcasted_iota(jnp.int32, (BLOCK, 2 * LANES), 1)
    return (lane & (LANES - 1)) // group_ch


def tail_kernel(k_hbm, v_hbm, tail_ref, k_ref, v_ref, sems):
    rows = pl.ds(k_hbm.shape[0] - tail_ref.shape[0], tail_ref.shape[0])
    for copy in fetch([(k_hbm.at[rows, :], k_ref), (v_hbm.at[rows, :], v_ref)], sems):
        copy.wait()
    tail_ref[...] = product_bf16(k_ref[...], v_ref[...])


def late_kernel(
    group_ch,
    k_hbm,
    v_hbm,
    q_hbm,
    gate_hbm,
    filter_hbm,
    gain_hbm,
    rates_hbm,
    tap_ref,
    u_ref,
    q_early_ref,
    gate_early_ref,
    gain_ref,
    step_ref,
    value_ref,
    square_ref,
    k_ref,
    v_ref,
    q_ref,
    gate_ref,
    filter_ref,
    rates_ref,
    sems,
):
    length, channels = k_hbm.shape
    half = length // 2
    early, late = pl.ds(0, half), pl.ds(half, half)
    copies = fetch(
        [
            (filter_hbm, filter_ref),
            (k_hbm, k_ref),
            (v_hbm, v_ref),
            (q_hbm.at[late, :], q_ref),
            (gate_hbm.at[late, :], gate_ref),
            (gain_hbm, gain_ref),
            (rates_hbm, rates_ref),
            (q_hbm.at[early, :], q_early_ref),
            (gate_hbm.at[early, :], gate_early_ref),
        ],
        sems,
    )
    copies[0].wait()
    groups, taps = filter_ref.shape
    row = lax.broadcasted_iota(jnp.int32, (taps, taps), 0)
    col = lax.broadcasted_iota(jnp.int32, (taps, taps), 1)
    flip = jnp.where(((row + col) & (taps - 1)) == 0, 1.0, 0.0).astype(BF16)
    mirrored = jnp.dot(filter_ref[...], flip, preferred_element_type=F32)
    before = (col > row)[:BLOCK]
    for group in range(groups):
        line = jnp.broadcast_to(mirrored[group : group + 1, :], (BLOCK, taps))
        circulant = pltpu.roll(line, 0, axis=1, stride=1, stride_axis=0)
        tap_ref[group, :, :taps] = jnp.where(before, circulant, 0.0).astype(BF16)
        tap_ref[group, :, taps:] = jnp.where(before, 0.0, circulant).astype(BF16)
    for copy in copies[1:7]:
        copy.wait()
    channel_rows(step_ref, jnp.exp(-rates_ref[...]))
    member = lane_member(group_ch)
    partial = [jnp.zeros((BLOCK, LANES), F32) for _ in range(2)]
    none = jnp.zeros((BLOCK, LANES), BF16)
    for tile in range(channels // LANES):
        cols = slice(tile * LANES, (tile + 1) * LANES)
        u_one = product_bf16(k_ref[:, cols], v_ref[:, cols])
        u_ref[:, cols] = u_one[:half]
        later = jnp.concatenate([u_one[BLOCK:], none], axis=0)
        windows = jnp.concatenate([u_one, later], axis=1)
        conv = filtered(tap_ref, tile, LANES // group_ch, windows, member)
        gated(conv, tile, q_ref[:, cols], gate_ref[:, cols], gain_ref[:, cols], partial, value_ref)
    square_ref[...] = token_row(partial)
    for copy in copies[7:]:
        copy.wait()


def early_kernel(
    group_ch,
    halo_ref,
    tap_ref,
    u_ref,
    q_ref,
    gate_ref,
    gain_ref,
    late_ref,
    value_ref,
    square_ref,
):
    member = lane_member(group_ch)
    partial = [jnp.zeros((BLOCK, LANES), F32) for _ in range(2)]
    none = jnp.zeros((BLOCK, LANES), BF16)
    for tile in range(u_ref.shape[1] // LANES):
        cols = slice(tile * LANES, (tile + 1) * LANES)
        halo, u_one = halo_ref[:, cols], u_ref[:, cols]
        first = jnp.concatenate([halo, u_one], axis=0)
        second = jnp.concatenate([halo[BLOCK:], u_one, none], axis=0)
        windows = jnp.concatenate([first, second], axis=1)
        conv = filtered(tap_ref, tile, LANES // group_ch, windows, member)
        gated(conv, tile, q_ref[:, cols], gate_ref[:, cols], gain_ref[:, cols], partial, value_ref)
    line = token_row(partial)
    for copy in range(square_ref.shape[0]):
        square_ref[copy, 0:1, :] = line
        square_ref[copy, 1:2, :] = late_ref[...]


def mode_rows(ref):
    return [ref[at : at + ROWS, :] for at in range(0, ref.shape[0], ROWS)]


def token_rows(t):
    return pl.ds(pl.multiple_of(t * ROWS, ROWS), ROWS)


def tree_sum(terms):
    while len(terms) > 1:
        terms = [x + y for x, y in zip(terms[::2], terms[1::2])]
    return terms[0]


def state_kernel(width, square_ref, early_ref, late_ref, step_ref, u_ref, state_ref, scale_ref):
    total = square_ref[0]
    for peer in range(1, square_ref.shape[0]):
        total = total + square_ref[peer]
    scale = lax.rsqrt(total / width + 1e-06)
    for part in range(2):
        line = jnp.broadcast_to(scale[part : part + 1, :], (LANES, LANES))
        scale_ref[part * LANES : (part + 1) * LANES, :] = line.T
    steps = mode_rows(step_ref)
    states = tuple(jnp.zeros((ROWS, LANES), F32) for _ in steps)
    for part, value_ref in enumerate((early_ref, late_ref)):

        def token(t, states):
            place = t + part * LANES
            factor = jnp.broadcast_to(scale_ref[pl.ds(place, 1), :], (ROWS, LANES))
            u_two = (value_ref[token_rows(t), :] * factor).astype(BF16).astype(F32)
            u_ref[token_rows(place), :] = u_two
            return tuple(a * s + u_two for a, s in zip(steps, states))

        states = lax.fori_loop(0, LANES, token, states, unroll=UNROLL)
    for m, state in enumerate(states):
        state_ref[m * ROWS : (m + 1) * ROWS, :] = state


def inner_kernel(
    share,
    place_ref,
    u_ref,
    step_ref,
    rates_hbm,
    residues_hbm,
    conv_ref,
    weight_ref,
    decay_ref,
    rates_ref,
    residues_ref,
    decays_ref,
    sems,
):
    for copy in fetch([(rates_hbm, rates_ref), (residues_hbm, residues_ref)], sems):
        copy.wait()
    rates = rates_ref[...]
    tokens = u_ref.shape[0] // ROWS
    channel_rows(decays_ref, jnp.exp(-rates * float(tokens)))
    decay_ref[...] = decays_ref[pl.ds(place_ref[0] * share, share), :]
    channel_rows(weight_ref, residues_ref[...] * jnp.sqrt(one_minus_exp(2.0 * rates)))
    steps, weights = mode_rows(step_ref), mode_rows(weight_ref)

    def token(t, states):
        u_two = u_ref[token_rows(t), :]
        states = tuple(a * s + u_two for a, s in zip(steps, states))
        conv_ref[token_rows(t), :] = tree_sum([w * s for w, s in zip(weights, states)])
        return states

    zero = tuple(jnp.zeros((ROWS, LANES), F32) for _ in steps)
    lax.fori_loop(0, tokens, token, zero, unroll=UNROLL)


def scan_kernel(state_ref, decay_ref, entry_ref):
    decay = decay_ref[...]
    entry = jnp.zeros_like(decay)
    for device in range(state_ref.shape[0]):
        entry_ref[device] = entry
        entry = decay * entry + state_ref[device]


def output_kernel(
    entry_ref, conv_ref, step_ref, weight_ref, gate_ref, out_hbm, sum_ref, out_ref, sems
):
    steps = mode_rows(step_ref)
    carried = tuple(w * e for w, e in zip(mode_rows(weight_ref), mode_rows(entry_ref)))
    length, channels = gate_ref.shape

    def advance(chunk, carried):
        for t in range(CHUNK):
            carried = tuple(a * e for a, e in zip(steps, carried))
            at = token_rows(chunk * CHUNK + t)
            sum_ref[at, :] = conv_ref[at, :] + tree_sum(list(carried))
        return carried

    def emit(chunk):
        rows = pl.ds(pl.multiple_of(chunk * CHUNK, CHUNK), CHUNK)
        for tile in range(channels // LANES):
            cols = slice(tile * LANES, (tile + 1) * LANES)
            conv_two = sum_ref[pl.ds(chunk * (CHUNK * ROWS) + tile, CHUNK, stride=ROWS), :]
            out_ref[rows, cols] = (gate_ref[rows, cols].astype(F32) * conv_two).astype(BF16)

    def both(chunk, carried):
        emit(chunk - 1)
        return advance(chunk, carried)

    chunks = length // CHUNK
    per_quarter = chunks // QUARTERS
    copies = []
    carried = advance(0, carried)
    for quarter in range(QUARTERS):
        last = (quarter + 1) * per_quarter
        first = quarter * per_quarter + 1
        carried = lax.fori_loop(first, min(last + 1, chunks), both, carried)
        if last == chunks:
            emit(chunks - 1)
        rows = pl.ds(quarter * per_quarter * CHUNK, per_quarter * CHUNK)
        copy = pltpu.make_async_copy(out_ref.at[rows, :], out_hbm.at[rows, :], sems.at[quarter])
        copy.start()
        copies.append(copy)
    for copy in copies:
        copy.wait()


def on_device(q_one, k_one, v_one, mr_filter, norm_gain, q_two, k_two, li_rates, li_residues):
    length, channels = q_one.shape
    groups, taps = mr_filter.shape
    modes = li_rates.shape[0]
    devices, peers = lax.axis_size("ctx"), lax.axis_size("tp")
    group_ch = channels // groups
    half = length // 2
    flat = (modes * ROWS, LANES)
    shares = (devices, flat[0] // devices, LANES)
    place = lax.axis_index("ctx").astype(jnp.int32).reshape(1)

    (tail,) = call(
        "tail",
        tail_kernel,
        [(IN_HBM, k_one), (IN_HBM, v_one)],
        [(IN_VMEM, (taps, channels), BF16)],
        [pltpu.VMEM((taps, channels), BF16)] * 2 + [pltpu.SemaphoreType.DMA((2,))],
    )
    halo = lax.ppermute(tail, "ctx", [(i, i + 1) for i in range(devices - 1)])
    late = call(
        "late",
        functools.partial(late_kernel, group_ch),
        [
            (IN_HBM, k_one),
            (IN_HBM, v_one),
            (IN_HBM, q_one),
            (IN_HBM, k_two),
            (IN_HBM, mr_filter),
            (IN_HBM, norm_gain[None, :]),
            (IN_HBM, li_rates),
        ],
        [
            (IN_VMEM, (groups, BLOCK, 2 * taps), BF16),
            (IN_VMEM, (half, channels), BF16),
            (IN_VMEM, (half, channels), BF16),
            (IN_VMEM, (half, channels), BF16),
            (IN_VMEM, (1, channels), F32),
            (IN_VMEM, flat, F32),
            (IN_VMEM, (half * ROWS, LANES), F32),
            (IN_VMEM, (1, half), F32),
        ],
        [
            pltpu.VMEM((length, channels), BF16),
            pltpu.VMEM((length, channels), BF16),
            pltpu.VMEM((half, channels), BF16),
            pltpu.VMEM((half, channels), BF16),
            pltpu.VMEM((groups, taps), BF16),
            pltpu.VMEM((modes, channels), F32),
            pltpu.SemaphoreType.DMA((9,)),
        ],
    )
    tap_table, u_early, q_early, gate_early, gain, steps, value_late, square_late = late
    value_early, squares = call(
        "early",
        functools.partial(early_kernel, group_ch),
        [
            (IN_VMEM, array)
            for array in (halo, tap_table, u_early, q_early, gate_early, gain, square_late)
        ],
        [(IN_VMEM, (half * ROWS, LANES), F32), (IN_VMEM, (peers, 2, LANES), F32)],
    )
    squares = lax.all_to_all(squares, "tp", split_axis=0, concat_axis=0, tiled=True)
    u_two, states = call(
        "states",
        functools.partial(state_kernel, float(channels * peers)),
        [(IN_VMEM, array) for array in (squares, value_early, value_late, steps)],
        [(IN_VMEM, (length * ROWS, LANES), F32), (IN_VMEM, flat, F32)],
        [pltpu.VMEM((length, LANES), F32)],
    )
    received = lax.all_to_all(
        states.reshape(shares), "ctx", split_axis=0, concat_axis=0, tiled=True
    )
    conv_inner, mode_weights, decay = call(
        "inner",
        functools.partial(inner_kernel, shares[1]),
        [
            (IN_SMEM, place),
            (IN_VMEM, u_two),
            (IN_VMEM, steps),
            (IN_HBM, li_rates),
            (IN_HBM, li_residues),
        ],
        [
            (IN_VMEM, (length * ROWS, LANES), F32),
            (IN_VMEM, flat, F32),
            (IN_VMEM, shares[1:], F32),
        ],
        [
            pltpu.VMEM((modes, channels), F32),
            pltpu.VMEM((modes, channels), F32),
            pltpu.VMEM(flat, F32),
            pltpu.SemaphoreType.DMA((2,)),
        ],
    )
    (entries,) = call(
        "scan",
        scan_kernel,
        [(IN_VMEM, received), (IN_VMEM, decay)],
        [(IN_VMEM, shares, F32)],
    )
    entries = lax.all_to_all(entries, "ctx", split_axis=0, concat_axis=0, tiled=True)
    (mixed,) = call(
        "output",
        output_kernel,
        [
            (IN_VMEM, array)
            for array in (entries.reshape(flat), conv_inner, steps, mode_weights, q_two)
        ],
        [(IN_HBM, (length, channels), BF16)],
        [
            pltpu.VMEM((length * ROWS, LANES), F32),
            pltpu.VMEM((length, channels), BF16),
            pltpu.SemaphoreType.DMA((QUARTERS,)),
        ],
    )
    return mixed


def solution(mesh):
    in_specs = (
        P("ctx", "tp"),
        P("ctx", "tp"),
        P("ctx", "tp"),
        P("tp", None),
        P("tp"),
        P("ctx", "tp"),
        P("ctx", "tp"),
        P(None, "tp"),
        P(None, "tp"),
    )
    return jax.shard_map(
        on_device, mesh=mesh, in_specs=in_specs, out_specs=P("ctx", "tp"), check_vma=False
    )
```

time: 81.9 us -> 69.3 us (0.85)
  Pallas kernels: 19.3 us -> 13.6 us
  blocking collectives: 31.8 us -> 28.9 us
  other arithmetic: 2.64 us -> 0 us
  starting transfers between devices: 16.6 us -> 18.6 us
  waiting for transfers between devices: 9.77 us -> 7.83 us
  local copies, waits for them, and re-layouts: 1.33 us -> 0.01 us
    pallas_call x5 -> x7, Pallas kernels: 19.3 us -> 13.6 us  [call(): pl.pallas_call(kernel, out_shape=[jax.ShapeDtypeStruct(dims, kind) for _,...]
    all_to_all x1, waiting for transfers between devices: 9.77 us -> 6.48 us  [on_device(): lax.all_to_all(states.reshape(shares), 'ctx', split_axis=0, concat_axis=0...]
    all_to_all x1, starting transfers between devices: 12 us -> 14.1 us  [on_device(): lax.all_to_all(states.reshape(shares), 'ctx', split_axis=0, concat_axis=0...]
    mul x1 -> x0, other arithmetic: 1.55 us -> none  [on_device(): weights = li_residues * jnp.sqrt(-jnp.expm1(-2.0 * li_rates))]
    all_to_all x1, blocking collectives: 15.1 us -> 13.6 us  [on_device(): lax.all_to_all(entries, 'ctx', split_axis=0, concat_axis=0, tiled=True)]
    all_to_all x1, blocking collectives: 16.7 us -> 15.3 us  [on_device(): lax.all_to_all(squares, 'tp', split_axis=0, concat_axis=0, tiled=True)]
    ppermute x1, waiting for transfers between devices: 0.01 us -> 1.35 us  [on_device(): halo = lax.ppermute(tail, 'ctx', [(i, i + 1) for i in range(devices - 1)])]
    unnamed x4 -> x2, local copies, waits for them, and re-layouts: 1.33 us -> 0.01 us
  transfers between devices with their start and end apart: 2 -> 2, of which waited for: 1 -> 2; matrix products, arithmetic and copies ran while one was open for 2% -> 0% of each run, Pallas kernels for 5% -> 9%
where the time goes in v2:
time: 69.3 us; the launch traced here: 69 us
  blocking collectives  28.9 us (42%)
  starting transfers between devices  18.6 us (27%)
  Pallas kernels  13.6 us (20%)
  waiting for transfers between devices  7.83 us (11%)
    all_to_all x1, blocking collectives, on_device(): lax.all_to_all(squares, 'tp', split_axis=0, concat_axis=0, tiled=True)  15.3 us
    all_to_all x1, starting transfers between devices, on_device(): lax.all_to_all(states.reshape(shares), 'ctx', split_axis=0, concat_axis=0...  14.1 us
    all_to_all x1, blocking collectives, on_device(): lax.all_to_all(entries, 'ctx', split_axis=0, concat_axis=0, tiled=True)  13.6 us
    pallas_call x7, Pallas kernels, call(): pl.pallas_call(kernel, out_shape=[jax.ShapeDtypeStruct(dims, kind) for _,...  13.6 us
    all_to_all x1, waiting for transfers between devices, on_device(): lax.all_to_all(states.reshape(shares), 'ctx', split_axis=0, concat_axis=0...  6.48 us
    ppermute x1, starting transfers between devices, on_device(): halo = lax.ppermute(tail, 'ctx', [(i, i + 1) for i in range(devices - 1)])  4.58 us
  transfers between devices with their start and end apart: 2, of which 2 were waited for; matrix products, arithmetic and copies ran while one was open for 0% of the time, Pallas kernels for 9%

profile of v2, /device:TPU:1, one launch (start us, length us, event | category | flops | bytes accessed | tf_op | source)
XLA Modules:
  0.0 69.0 jit_solution(5178062556125122088)
XLA Ops:
  0.0 1.1 %tail.1 = bf16[128,1024]{1,0:T(8,128)(2,1)S(1)} custom-call(bf16[256,1024]{1,0:T(8,128)(2,1)} %k_hbm.3, bf16[256,1024]{1,0:T(8,128)(2,1)} %v_hbm.3), custom_call_target="tpu_custom_call" | custom-call | tf_op jit(solution)/shard_map/tail/pallas_call | solution.py:29
  1.1 4.6 %collective-permute-start = (bf16[128,1024]{1,0:T(8,128)(2,1)S(1)}, bf16[128,1024]{1,0:T(8,128)(2,1)S(1)}, u32[]{:S(2)}, u32[]{:S(2)}) collective-permute-start(bf16[128,1024]{1,0:T(8,128)(2,1)S(1)} %tail.1), channel_id=1, source_target_pairs={{0,8},{8,16},{16,24},{24,32},{32,40},{40,48},{48,56},{56,64},{64,7... | collective-permute-start | bytes 786440 | tf_op jit(solution)/shard_map/ppermute | solution.py:345
  5.7 3.2 %late.1 = (bf16[64,64,256]{2,1,0:T(8,128)(2,1)S(1)}, bf16[128,1024]{1,0:T(8,128)(2,1)S(1)}, bf16[128,1024]{1,0:T(8,128)(2,1)S(1)}, bf16[128,1024]{1,0:T(8,128)(2...) custom-call(bf16[256,1024]{1,0:T(8,128)(2,1)} %k_hbm.3, ...), custom_call_target="tpu_custom_call" | custom-call | tf_op jit(solution)/shard_map/late/pallas_call | solution.py:29
  8.9 1.3 %collective-permute-done.halo_ref = bf16[128,1024]{1,0:T(8,128)(2,1)S(1)} collective-permute-done((bf16[128,1024]{1,0:T(8,128)(2,1)S(1)}, bf16[128,1024]{1,0:T(8,128)(2,1)S(1)}, u32[]{:S(2)}, u32[]{:S(2)}) %collective-permute-start) | collective-permute-done | bytes 262176 | tf_op jit(solution)/shard_map/ppermute | solution.py:345
  10.3 1.7 %early.1 = (f32[1024,128]{1,0:T(8,128)S(1)}, f32[8,2,128]{2,1,0:T(2,128)S(1)}) custom-call(bf16[128,1024]{1,0:T(8,128)(2,1)S(1)} %collective-permute-done.halo_ref, bf16[64,64,256]{2,1,0:T(8,128)(2,1)S(1)} %get-tuple-element.20.tap_ref, bf16[128,1024]{1,0:T(8,128)(2,1)S(1)} %get-tuple-element.21.u_ref, bf16[128,1024]{1,0:T(8,128)(2,1)S(1)} %get-tuple-element.22.q_ref, ...), custom_call_target="tpu_custom_call" | custom-call | tf_op jit(solution)/shard_map/early/pallas_call | solution.py:29
  12.0 0.0 copy-start
  12.0 15.3 %all_to_all.15.square_ref = f32[8,2,128]{2,1,0:T(2,128)S(1)} all-to-all(f32[8,2,128]{2,1,0:T(2,128)S(1)} %get-tuple-element.26), channel_id=1, replica_groups=mesh['ctx'=64,'tp'=8] {'tp'}, dimensions={0} | all-to-all | bytes 16384 | tf_op jit(solution)/shard_map/all_to_all | solution.py:388
  27.3 2.1 %states.1 = (f32[2048,128]{1,0:T(8,128)S(1)}, f32[128,128]{1,0:T(8,128)}) custom-call(f32[8,2,128]{2,1,0:T(2,128)S(1)} %all_to_all.15.square_ref, f32[1024,128]{1,0:T(8,128)S(1)} %get-tuple-element.27.early_ref, f32[1024,128]{1,0:T(8,128)S(1)} %get-tuple-element.28.late_ref, f32[128,128]{1,0:T(8,128)S(1)} %get-tuple-element.29.step_ref), custom_call_target="tpu_custom_call" | custom-call | tf_op jit(solution)/shard_map/states/pallas_call | solution.py:29
  29.3 14.1 %all-to-all-start.1 = ((f32[64,2,128]{2,1,0:T(2,128)}), f32[64,2,128]{2,1,0:T(2,128)S(1)}, u32[]{:S(2)}, u32[]{:S(2)}) async-start(f32[64,2,128]{2,1,0:T(2,128)} %bitcast.1), calls=%async_computation.1 | async-start | bytes 131072 | tf_op jit(solution)/shard_map/all_to_all | solution.py:396
  43.4 3.3 %inner.1 = (f32[2048,128]{1,0:T(8,128)S(1)}, f32[128,128]{1,0:T(8,128)S(1)}, f32[2,128]{1,0:T(2,128)S(1)}) custom-call(s32[1]{0:T(128)} %bitcast.2.place_ref, f32[2048,128]{1,0:T(8,128)S(1)} %get-tuple-element.31.u_ref, f32[128,128]{1,0:T(8,128)S(1)} %get-tuple-element.29.step_ref, f32[16,1024]{1,0:T(8,128)} %rates_hbm.3, f32[16,1024]{1,0:T(8,128)} %residues_hbm.1), custom_call_target="tpu_custom_call" | custom-call | tf_op jit(solution)/shard_map/inner/pallas_call | solution.py:29
  46.7 6.5 %all-to-all-done.1.state_ref = f32[64,2,128]{2,1,0:T(2,128)S(1)} async-done(((f32[64,2,128]{2,1,0:T(2,128)}), f32[64,2,128]{2,1,0:T(2,128)S(1)}, u32[]{:S(2)}, u32[]{:S(2)}) %all-to-all-start.1) | async-done | bytes 65568 | tf_op jit(solution)/shard_map/all_to_all | solution.py:396
  53.2 0.1 scan.1
  53.3 13.6 %all_to_all.16 = f32[64,2,128]{2,1,0:T(2,128)S(1)} all-to-all(f32[64,2,128]{2,1,0:T(2,128)S(1)} %scan.1), channel_id=1, replica_groups=mesh['ctx'=64,'tp'=8] {'ctx'}, dimensions={0} | all-to-all | bytes 131072 | tf_op jit(solution)/shard_map/all_to_all | solution.py:427
  66.9 0.0 copy-done
  66.9 2.1 %output.1 = bf16[256,1024]{1,0:T(8,128)(2,1)} custom-call(f32[128,128]{1,0:T(8,128)S(1)} %bitcast.4, f32[2048,128]{1,0:T(8,128)S(1)} %get-tuple-element.33.conv_ref, f32[128,128]{1,0:T(8,128)S(1)} %get-tuple-element.29.step_ref, f32[128,128]{1,0:T(8,128)S(1)} %get-tuple-element.34.weight_ref, bf16[256,1024]{1,0:T(8,128)(2,1)S(1)} %copy-done), custom_call_target="tpu_custom_call" | custom-call | tf_op jit(solution)/shard_map/output/pallas_call | solution.py:29
Async XLA Ops:
  1.1 9.1 %collective-permute-start = (bf16[128,1024]{1,0:T(8,128)(2,1)S(1)}, bf16[128,1024]{1,0:T(8,128)(2,1)S(1)}, u32[]{:S(2)}, u32[]{:S(2)}) collective-permute-start(bf16[128,1024]{1,0:T(8,128)(2,1)S(1)} %tail.1), channel_id=1, source_target_pairs={{0,8},{8,16},{16,24},{24,32},{32,40},{40,48},{48,56},{56,64},{64,7... | collective-permute-start | bytes 786440 | tf_op jit(solution)/shard_map/ppermute | solution.py:345
  12.0 54.9 %copy-start = (bf16[256,1024]{1,0:T(8,128)(2,1)S(1)}, bf16[256,1024]{1,0:T(8,128)(2,1)}, u32[]{:S(2)}) copy-start(bf16[256,1024]{1,0:T(8,128)(2,1)} %gate_ref.1) | copy-start | bytes 1572868
  29.3 23.8 %all-to-all-start.1 = ((f32[64,2,128]{2,1,0:T(2,128)}), f32[64,2,128]{2,1,0:T(2,128)S(1)}, u32[]{:S(2)}, u32[]{:S(2)}) async-start(f32[64,2,128]{2,1,0:T(2,128)} %bitcast.1), calls=%async_computation.1 | async-start | bytes 131072 | tf_op jit(solution)/shard_map/all_to_all | solution.py:396

commit v3 on v2

--- a/solution.py
+++ b/solution.py
@@ -69,7 +69,8 @@
 def filtered(tap_ref, tile, per_tile, windows, member):
     conv = None
     for place in range(per_tile):
-        product = jnp.dot(tap_ref[tile * per_tile + place], windows, preferred_element_type=F32)
+        taps = tap_ref[tile * per_tile + place, :, : windows.shape[0]]
+        product = jnp.dot(taps, windows, preferred_element_type=F32)
         conv = product if place == 0 else jnp.where(member == place, product, conv)
     return conv
 
@@ -101,6 +102,8 @@
 
 def late_kernel(
     group_ch,
+    share,
+    place_ref,
     k_hbm,
     v_hbm,
     q_hbm,
@@ -108,12 +111,15 @@
     filter_hbm,
     gain_hbm,
     rates_hbm,
+    residues_hbm,
     tap_ref,
-    u_ref,
+    conv_ref,
     q_early_ref,
     gate_early_ref,
     gain_ref,
     step_ref,
+    weight_ref,
+    decay_ref,
     value_ref,
     square_ref,
     k_ref,
@@ -122,6 +128,8 @@
     gate_ref,
     filter_ref,
     rates_ref,
+    residues_ref,
+    decays_ref,
     sems,
 ):
     length, channels = k_hbm.shape
@@ -136,6 +144,7 @@
             (gate_hbm.at[late, :], gate_ref),
             (gain_hbm, gain_ref),
             (rates_hbm, rates_ref),
+            (residues_hbm, residues_ref),
             (q_hbm.at[early, :], q_early_ref),
             (gate_hbm.at[early, :], gate_early_ref),
         ],
@@ -153,22 +162,29 @@
         circulant = pltpu.roll(line, 0, axis=1, stride=1, stride_axis=0)
         tap_ref[group, :, :taps] = jnp.where(before, circulant, 0.0).astype(BF16)
         tap_ref[group, :, taps:] = jnp.where(before, 0.0, circulant).astype(BF16)
-    for copy in copies[1:7]:
+    for copy in copies[1:8]:
         copy.wait()
-    channel_rows(step_ref, jnp.exp(-rates_ref[...]))
+    rates = rates_ref[...]
+    channel_rows(step_ref, jnp.exp(-rates))
+    channel_rows(decays_ref, jnp.exp(-rates * float(length)))
+    channel_rows(weight_ref, residues_ref[...] * jnp.sqrt(one_minus_exp(2.0 * rates)))
+    decay_ref[...] = decays_ref[pl.ds(place_ref[0] * share, share), :]
     member = lane_member(group_ch)
     partial = [jnp.zeros((BLOCK, LANES), F32) for _ in range(2)]
     none = jnp.zeros((BLOCK, LANES), BF16)
     for tile in range(channels // LANES):
         cols = slice(tile * LANES, (tile + 1) * LANES)
         u_one = product_bf16(k_ref[:, cols], v_ref[:, cols])
-        u_ref[:, cols] = u_one[:half]
+        first = jnp.concatenate([none, none, u_one[:half]], axis=0)
+        second = jnp.concatenate([none, u_one[: half + BLOCK]], axis=0)
+        windows = jnp.concatenate([first, second], axis=1)
+        conv_ref[tile] = filtered(tap_ref, tile, LANES // group_ch, windows, member)
         later = jnp.concatenate([u_one[BLOCK:], none], axis=0)
         windows = jnp.concatenate([u_one, later], axis=1)
         conv = filtered(tap_ref, tile, LANES // group_ch, windows, member)
         gated(conv, tile, q_ref[:, cols], gate_ref[:, cols], gain_ref[:, cols], partial, value_ref)
     square_ref[...] = token_row(partial)
-    for copy in copies[7:]:
+    for copy in copies[8:]:
         copy.wait()
 
 
@@ -176,7 +192,7 @@
     group_ch,
     halo_ref,
     tap_ref,
-    u_ref,
+    conv_ref,
     q_ref,
     gate_ref,
     gain_ref,
@@ -187,13 +203,12 @@
     member = lane_member(group_ch)
     partial = [jnp.zeros((BLOCK, LANES), F32) for _ in range(2)]
     none = jnp.zeros((BLOCK, LANES), BF16)
-    for tile in range(u_ref.shape[1] // LANES):
+    for tile in range(halo_ref.shape[1] // LANES):
         cols = slice(tile * LANES, (tile + 1) * LANES)
-        halo, u_one = halo_ref[:, cols], u_ref[:, cols]
-        first = jnp.concatenate([halo, u_one], axis=0)
-        second = jnp.concatenate([halo[BLOCK:], u_one, none], axis=0)
-        windows = jnp.concatenate([first, second], axis=1)
-        conv = filtered(tap_ref, tile, LANES // group_ch, windows, member)
+        halo = halo_ref[:, cols]
+        second = jnp.concatenate([halo[BLOCK:], none], axis=0)
+        windows = jnp.concatenate([halo, second], axis=1)
+        conv = conv_ref[tile] + filtered(tap_ref, tile, LANES // group_ch, windows, member)
         gated(conv, tile, q_ref[:, cols], gate_ref[:, cols], gain_ref[:, cols], partial, value_ref)
     line = token_row(partial)
     for copy in range(square_ref.shape[0]):
@@ -239,38 +254,19 @@
         state_ref[m * ROWS : (m + 1) * ROWS, :] = state
 
 
-def inner_kernel(
-    share,
-    place_ref,
-    u_ref,
-    step_ref,
-    rates_hbm,
-    residues_hbm,
-    conv_ref,
-    weight_ref,
-    decay_ref,
-    rates_ref,
-    residues_ref,
-    decays_ref,
-    sems,
-):
-    for copy in fetch([(rates_hbm, rates_ref), (residues_hbm, residues_ref)], sems):
-        copy.wait()
-    rates = rates_ref[...]
-    tokens = u_ref.shape[0] // ROWS
-    channel_rows(decays_ref, jnp.exp(-rates * float(tokens)))
-    decay_ref[...] = decays_ref[pl.ds(place_ref[0] * share, share), :]
-    channel_rows(weight_ref, residues_ref[...] * jnp.sqrt(one_minus_exp(2.0 * rates)))
+def inner_kernel(u_ref, step_ref, weight_ref, decay_ref, conv_ref, decay_copy_ref):
+    decay_copy_ref[...] = decay_ref[...]
     steps, weights = mode_rows(step_ref), mode_rows(weight_ref)
 
     def token(t, states):
-        u_two = u_ref[token_rows(t), :]
+        at = token_rows(t)
+        u_two = u_ref[at, :]
         states = tuple(a * s + u_two for a, s in zip(steps, states))
-        conv_ref[token_rows(t), :] = tree_sum([w * s for w, s in zip(weights, states)])
+        conv_ref[at, :] = tree_sum([w * s for w, s in zip(weights, states)])
         return states
 
     zero = tuple(jnp.zeros((ROWS, LANES), F32) for _ in steps)
-    lax.fori_loop(0, tokens, token, zero, unroll=UNROLL)
+    lax.fori_loop(0, u_ref.shape[0] // ROWS, token, zero, unroll=UNROLL)
 
 
 def scan_kernel(state_ref, decay_ref, entry_ref):
@@ -286,7 +282,7 @@
 ):
     steps = mode_rows(step_ref)
     carried = tuple(w * e for w, e in zip(mode_rows(weight_ref), mode_rows(entry_ref)))
-    length, channels = gate_ref.shape
+    length, channels = out_ref.shape
 
     def advance(chunk, carried):
         for t in range(CHUNK):
@@ -345,8 +341,9 @@
     halo = lax.ppermute(tail, "ctx", [(i, i + 1) for i in range(devices - 1)])
     late = call(
         "late",
-        functools.partial(late_kernel, group_ch),
-        [
+        functools.partial(late_kernel, group_ch, shares[1]),
+        [
+            (IN_SMEM, place),
             (IN_HBM, k_one),
             (IN_HBM, v_one),
             (IN_HBM, q_one),
@@ -354,14 +351,17 @@
             (IN_HBM, mr_filter),
             (IN_HBM, norm_gain[None, :]),
             (IN_HBM, li_rates),
+            (IN_HBM, li_residues),
         ],
         [
             (IN_VMEM, (groups, BLOCK, 2 * taps), BF16),
-            (IN_VMEM, (half, channels), BF16),
+            (IN_VMEM, (channels // LANES, BLOCK, 2 * LANES), F32),
             (IN_VMEM, (half, channels), BF16),
             (IN_VMEM, (half, channels), BF16),
             (IN_VMEM, (1, channels), F32),
             (IN_VMEM, flat, F32),
+            (IN_VMEM, flat, F32),
+            (IN_VMEM, shares[1:], F32),
             (IN_VMEM, (half * ROWS, LANES), F32),
             (IN_VMEM, (1, half), F32),
         ],
@@ -372,16 +372,19 @@
             pltpu.VMEM((half, channels), BF16),
             pltpu.VMEM((groups, taps), BF16),
             pltpu.VMEM((modes, channels), F32),
-            pltpu.SemaphoreType.DMA((9,)),
-        ],
-    )
-    tap_table, u_early, q_early, gate_early, gain, steps, value_late, square_late = late
+            pltpu.VMEM((modes, channels), F32),
+            pltpu.VMEM(flat, F32),
+            pltpu.SemaphoreType.DMA((10,)),
+        ],
+    )
+    tap_table, conv_early, q_early, gate_early, gain, *late = late
+    steps, mode_weights, decay, value_late, square_late = late
     value_early, squares = call(
         "early",
         functools.partial(early_kernel, group_ch),
         [
             (IN_VMEM, array)
-            for array in (halo, tap_table, u_early, q_early, gate_early, gain, square_late)
+            for array in (halo, tap_table, conv_early, q_early, gate_early, gain, square_late)
         ],
         [(IN_VMEM, (half * ROWS, LANES), F32), (IN_VMEM, (peers, 2, LANES), F32)],
     )
@@ -396,27 +399,11 @@
     received = lax.all_to_all(
         states.reshape(shares), "ctx", split_axis=0, concat_axis=0, tiled=True
     )
-    conv_inner, mode_weights, decay = call(
+    conv_inner, decay = call(
         "inner",
-        functools.partial(inner_kernel, shares[1]),
-        [
-            (IN_SMEM, place),
-            (IN_VMEM, u_two),
-            (IN_VMEM, steps),
-            (IN_HBM, li_rates),
-            (IN_HBM, li_residues),
-        ],
-        [
-            (IN_VMEM, (length * ROWS, LANES), F32),
-            (IN_VMEM, flat, F32),
-            (IN_VMEM, shares[1:], F32),
-        ],
-        [
-            pltpu.VMEM((modes, channels), F32),
-            pltpu.VMEM((modes, channels), F32),
-            pltpu.VMEM(flat, F32),
-            pltpu.SemaphoreType.DMA((2,)),
-        ],
+        inner_kernel,
+        [(IN_VMEM, array) for array in (u_two, steps, mode_weights, decay)],
+        [(IN_VMEM, (length * ROWS, LANES), F32), (IN_VMEM, shares[1:], F32)],
     )
     (entries,) = call(
         "scan",

time: 69.3 us -> 68.4 us (0.987)
  starting transfers between devices: 18.6 us -> 17.2 us
  blocking collectives: 28.9 us -> 30.1 us
    all_to_all x1, starting transfers between devices: 14.1 us -> 12.6 us  [on_device(): lax.all_to_all(states.reshape(shares), 'ctx', split_axis=0, concat_axis=0...]
    ppermute x1, waiting for transfers between devices: 1.35 us -> 0.01 us  [on_device(): halo = lax.ppermute(tail, 'ctx', [(i, i + 1) for i in range(devices - 1)])]
    all_to_all x1, blocking collectives: 15.3 us -> 16.6 us  [on_device(): lax.all_to_all(squares, 'tp', split_axis=0, concat_axis=0, tiled=True)]
    all_to_all x1, waiting for transfers between devices: 6.48 us -> 7.52 us  [on_device(): lax.all_to_all(states.reshape(shares), 'ctx', split_axis=0, concat_axis=0...]
  transfers between devices with their start and end apart: 2 -> 2, of which waited for: 2 -> 1; matrix products, arithmetic and copies ran while one was open for 0% -> 0% of each run, Pallas kernels for 9% -> 10%
where the time goes in v3:
time: 68.4 us; the launch traced here: 68.1 us
  blocking collectives  30.1 us (44%)
  starting transfers between devices  17.2 us (25%)
  Pallas kernels  13.2 us (19%)
  waiting for transfers between devices  7.52 us (11%)
    all_to_all x1, blocking collectives, on_device(): lax.all_to_all(squares, 'tp', split_axis=0, concat_axis=0, tiled=True)  16.6 us
    all_to_all x1, blocking collectives, on_device(): lax.all_to_all(entries, 'ctx', split_axis=0, concat_axis=0, tiled=True)  13.6 us
    pallas_call x7, Pallas kernels, call(): pl.pallas_call(kernel, out_shape=[jax.ShapeDtypeStruct(dims, kind) for _,...  13.2 us
    all_to_all x1, starting transfers between devices, on_device(): lax.all_to_all(states.reshape(shares), 'ctx', split_axis=0, concat_axis=0...  12.6 us
    all_to_all x1, waiting for transfers between devices, on_device(): lax.all_to_all(states.reshape(shares), 'ctx', split_axis=0, concat_axis=0...  7.52 us
    ppermute x1, starting transfers between devices, on_device(): halo = lax.ppermute(tail, 'ctx', [(i, i + 1) for i in range(devices - 1)])  4.58 us
  transfers between devices with their start and end apart: 2, of which 1 were waited for; matrix products, arithmetic and copies ran while one was open for 0% of the time, Pallas kernels for 10%

profile of v3, /device:TPU:1, one launch (start us, length us, event | category | flops | bytes accessed | tf_op | source)
XLA Modules:
  0.0 68.1 jit_solution(5973547182426565586)
XLA Ops:
  0.0 1.1 %tail.1 = bf16[128,1024]{1,0:T(8,128)(2,1)S(1)} custom-call(bf16[256,1024]{1,0:T(8,128)(2,1)} %k_hbm.3, bf16[256,1024]{1,0:T(8,128)(2,1)} %v_hbm.3), custom_call_target="tpu_custom_call" | custom-call | tf_op jit(solution)/shard_map/tail/pallas_call | solution.py:29
  1.1 4.6 %collective-permute-start = (bf16[128,1024]{1,0:T(8,128)(2,1)S(1)}, bf16[128,1024]{1,0:T(8,128)(2,1)S(1)}, u32[]{:S(2)}, u32[]{:S(2)}) collective-permute-start(bf16[128,1024]{1,0:T(8,128)(2,1)S(1)} %tail.1), channel_id=1, source_target_pairs={{0,8},{8,16},{16,24},{24,32},{32,40},{40,48},{48,56},{56,64},{64,7... | collective-permute-start | bytes 786440 | tf_op jit(solution)/shard_map/ppermute | solution.py:341
  5.7 4.7 %late.1 = (bf16[64,64,256]{2,1,0:T(8,128)(2,1)S(1)}, f32[8,64,256]{2,1,0:T(8,128)S(1)}, bf16[128,1024]{1,0:T(8,128)(2,1)S(1)}, bf16[128,1024]{1,0:T(8,128)(2,1)S...) custom-call(s32[1]{0:T(128)} %bitcast.place_ref, ...), custom_call_target="tpu_custom_call" | custom-call | tf_op jit(solution)/shard_map/late/pallas_call | solution.py:29
  10.5 0.0 collective-permute-done.halo_ref
  10.5 0.8 %early.1 = (f32[1024,128]{1,0:T(8,128)S(1)}, f32[8,2,128]{2,1,0:T(2,128)S(1)}) custom-call(bf16[128,1024]{1,0:T(8,128)(2,1)S(1)} %collective-permute-done.halo_ref, bf16[64,64,256]{2,1,0:T(8,128)(2,1)S(1)} %get-tuple-element.21.tap_ref, f32[8,64,256]{2,1,0:T(8,128)S(1)} %get-tuple-element.22.conv_ref, bf16[128,1024]{1,0:T(8,128)(2,1)S(1)} %get-tuple-element.23.q_ref, ...), custom_call_target="tpu_custom_call" | custom-call | tf_op jit(solution)/shard_map/early/pallas_call | solution.py:29
  11.3 0.0 copy-start
  11.3 16.6 %all_to_all.15.square_ref = f32[8,2,128]{2,1,0:T(2,128)S(1)} all-to-all(f32[8,2,128]{2,1,0:T(2,128)S(1)} %get-tuple-element.27), channel_id=1, replica_groups=mesh['ctx'=64,'tp'=8] {'tp'}, dimensions={0} | all-to-all | bytes 16384 | tf_op jit(solution)/shard_map/all_to_all | solution.py:391
  27.9 2.1 %states.1 = (f32[2048,128]{1,0:T(8,128)S(1)}, f32[128,128]{1,0:T(8,128)}) custom-call(f32[8,2,128]{2,1,0:T(2,128)S(1)} %all_to_all.15.square_ref, f32[1024,128]{1,0:T(8,128)S(1)} %get-tuple-element.28.early_ref, f32[1024,128]{1,0:T(8,128)S(1)} %get-tuple-element.29.late_ref, f32[128,128]{1,0:T(8,128)S(1)} %get-tuple-element.30.step_ref), custom_call_target="tpu_custom_call" | custom-call | tf_op jit(solution)/shard_map/states/pallas_call | solution.py:29
  30.0 12.6 %all-to-all-start.1 = ((f32[64,2,128]{2,1,0:T(2,128)}), f32[64,2,128]{2,1,0:T(2,128)S(1)}, u32[]{:S(2)}, u32[]{:S(2)}) async-start(f32[64,2,128]{2,1,0:T(2,128)} %bitcast.2), calls=%async_computation.1 | async-start | bytes 131072 | tf_op jit(solution)/shard_map/all_to_all | solution.py:399
  42.5 2.3 %inner.1 = (f32[2048,128]{1,0:T(8,128)S(1)}, f32[2,128]{1,0:T(2,128)S(1)}) custom-call(f32[2048,128]{1,0:T(8,128)S(1)} %get-tuple-element.32.u_ref, f32[128,128]{1,0:T(8,128)S(1)} %get-tuple-element.30.step_ref, f32[128,128]{1,0:T(8,128)S(1)} %get-tuple-element.33.weight_ref, f32[2,128]{1,0:T(2,128)S(1)} %get-tuple-element.34.decay_ref), custom_call_target="tpu_custom_call" | custom-call | tf_op jit(solution)/shard_map/inner/pallas_call | solution.py:29
  44.8 7.5 %all-to-all-done.1.state_ref = f32[64,2,128]{2,1,0:T(2,128)S(1)} async-done(((f32[64,2,128]{2,1,0:T(2,128)}), f32[64,2,128]{2,1,0:T(2,128)S(1)}, u32[]{:S(2)}, u32[]{:S(2)}) %all-to-all-start.1) | async-done | bytes 65568 | tf_op jit(solution)/shard_map/all_to_all | solution.py:399
  52.3 0.1 scan.1
  52.4 13.6 %all_to_all.16 = f32[64,2,128]{2,1,0:T(2,128)S(1)} all-to-all(f32[64,2,128]{2,1,0:T(2,128)S(1)} %scan.1), channel_id=1, replica_groups=mesh['ctx'=64,'tp'=8] {'ctx'}, dimensions={0} | all-to-all | bytes 131072 | tf_op jit(solution)/shard_map/all_to_all | solution.py:414
  66.0 0.0 copy-done
  66.0 2.1 %output.1 = bf16[256,1024]{1,0:T(8,128)(2,1)} custom-call(f32[128,128]{1,0:T(8,128)S(1)} %bitcast.4, f32[2048,128]{1,0:T(8,128)S(1)} %get-tuple-element.36.conv_ref, f32[128,128]{1,0:T(8,128)S(1)} %get-tuple-element.30.step_ref, f32[128,128]{1,0:T(8,128)S(1)} %get-tuple-element.33.weight_ref, bf16[256,1024]{1,0:T(8,128)(2,1)S(1)} %copy-done), custom_call_target="tpu_custom_call" | custom-call | tf_op jit(solution)/shard_map/output/pallas_call | solution.py:29
Async XLA Ops:
  1.1 9.4 %collective-permute-start = (bf16[128,1024]{1,0:T(8,128)(2,1)S(1)}, bf16[128,1024]{1,0:T(8,128)(2,1)S(1)}, u32[]{:S(2)}, u32[]{:S(2)}) collective-permute-start(bf16[128,1024]{1,0:T(8,128)(2,1)S(1)} %tail.1), channel_id=1, source_target_pairs={{0,8},{8,16},{16,24},{24,32},{32,40},{40,48},{48,56},{56,64},{64,7... | collective-permute-start | bytes 786440 | tf_op jit(solution)/shard_map/ppermute | solution.py:341
  11.3 54.7 %copy-start = (bf16[256,1024]{1,0:T(8,128)(2,1)S(1)}, bf16[256,1024]{1,0:T(8,128)(2,1)}, u32[]{:S(2)}) copy-start(bf16[256,1024]{1,0:T(8,128)(2,1)} %gate_ref.1) | copy-start | bytes 1572868
  30.0 22.4 %all-to-all-start.1 = ((f32[64,2,128]{2,1,0:T(2,128)}), f32[64,2,128]{2,1,0:T(2,128)S(1)}, u32[]{:S(2)}, u32[]{:S(2)}) async-start(f32[64,2,128]{2,1,0:T(2,128)} %bitcast.2), calls=%async_computation.1 | async-start | bytes 131072 | tf_op jit(solution)/shard_map/all_to_all | solution.py:399
